TPU v7x, 256 devices: a whole 4x4x8 slice. The times are simulated.
256 devices in a mesh: dp: 64 (over z, x, y_hi), tensor: 4 (over y_lo, core).
Axes of the slice: x: 4, y: 4 (y_hi: 2, y_lo: 2; y = y_hi * 2 + y_lo), z: 8, core: 2. Of those that a mesh axis runs over, the one named last changes fastest.
Arguments:
- inputs: float32 [64, 197, 768], P('dp')
- cotangent: float32 [64, 197, 768], P('dp'), may hold values from -6 to 6
- norm_gains: float32 [2, 768], P(None, 'dp'), may hold values from 0.5 to 1.5
- attn_mats: float32 [4, 768, 768], P(None, 'dp', 'tensor')
- router: float32 [768, 3], P('dp'), may hold values from -0.4375 to 0.4375
- expert_in: float32 [3, 768, 1536], P(None, 'dp', 'tensor'), may hold values from -0.21875 to 0.21875
- expert_out: float32 [3, 768, 1536], P(None, 'dp', 'tensor'), may hold values from -0.3125 to 0.3125
- moment_gains: float32 [2, 768], P(None, 'dp'), may hold values from -128 to 128
- moment_attn: float32 [4, 768, 768], P(None, 'dp', 'tensor'), may hold values from -32 to 32
- moment_router: float32 [768, 3], P('dp'), may hold values from -320 to 320
- moment_in: float32 [3, 768, 1536], P(None, 'dp', 'tensor'), may hold values from -32 to 32
- moment_out: float32 [3, 768, 1536], P(None, 'dp', 'tensor'), may hold values from -32 to 32
- routes: int32 [64, 197, 2], P('dp'), may hold values from 0 to 2, all different within a row; in each aligned block of 197 rows (0 to 196, 197 to 393, ..., all dimensions but the last counted through in order) at most 197 rows name the same one
Outputs:
- output: float32 [64, 197, 768], P('dp')
- grad_inputs: float32 [64, 197, 768], P('dp')
- grad_gains: float32 [2, 768], P(None, 'dp')
- grad_attn: float32 [4, 768, 768], P(None, 'dp', 'tensor')
- grad_router: float32 [768, 3], P('dp')
- grad_in: float32 [3, 768, 1536], P(None, 'dp', 'tensor')
- grad_out: float32 [3, 768, 1536], P(None, 'dp', 'tensor')
- gains_new: float32 [2, 768], P(None, 'dp')
- attn_new: float32 [4, 768, 768], P(None, 'dp', 'tensor')
- router_new: float32 [768, 3], P('dp')
- in_new: float32 [3, 768, 1536], P(None, 'dp', 'tensor')
- out_new: float32 [3, 768, 1536], P(None, 'dp', 'tensor')
- moment_gains_new: float32 [2, 768], P(None, 'dp')
- moment_attn_new: float32 [4, 768, 768], P(None, 'dp', 'tensor')
- moment_router_new: float32 [768, 3], P('dp')
- moment_in_new: float32 [3, 768, 1536], P(None, 'dp', 'tensor')
- moment_out_new: float32 [3, 768, 1536], P(None, 'dp', 'tensor')
Inputs may be any that keep to these rules, and one draw needn't show every extreme that they name: `routes`: in the rows of one index of dp no expert is named by more than 197 of them, a bound that some block reaches; a row's two experts differ.
All inputs are finite; a program needn't handle non-finite values.
Results may differ from a plain program's by a relative error of at most 0.025.
The roundings to bfloat16 on the way count: a program that leaves them out, or rounds other values in their place, can miss the bound.
Values may be sent and summed in bfloat16 or wider, within the bound.
A program may use at most 128 MiB of HBM per device.

v0:
```python
import math
import jax
import jax.numpy as jnp
import numpy as np
from jax import lax
from jax.sharding import PartitionSpec as P

HEAD_DIM = 64
EF = 3
NS_ITERS = 3
CAP = 197
EPSILON = 1e-06
MOMENTUM = 0.9
MUON_RATE = 0.5
SMALL_RATE = 0.5
NEWTON_A = 3.4445
NEWTON_B = -4.775
NEWTON_C = 2.0315
ROOT_HALF = 0.7071067811865476
INV_ROOT_TAU = 0.3989422804014327


def for_sending(value):
    return jax.tree.map(lambda a: a.astype(jnp.bfloat16) if a.dtype == jnp.float32 else a, value)


def round_half(operand):
    return operand.astype(jnp.bfloat16)


def settle(operand):
    return lax.optimization_barrier(operand.astype(jnp.bfloat16))


def to_single(operand):
    return operand.astype(jnp.float32)


def contract_rows(left_mat, right_mat):
    return lax.dot_general(
        left_mat, right_mat, (((0,), (0,)), ((), ())), preferred_element_type=jnp.float32
    )


def contract_cols(left_mat, right_mat):
    return lax.dot_general(
        left_mat, right_mat, (((1,), (1,)), ((), ())), preferred_element_type=jnp.float32
    )


def fold_sources(received, source_count):
    return jnp.sum(
        received.reshape((source_count, received.shape[0] // source_count) + received.shape[1:]),
        axis=0,
    )


def norm_forward(row_data, gain_row):
    center = row_data - jnp.mean(row_data, axis=-1, keepdims=True)
    inv_std = lax.rsqrt(jnp.mean(center * center, axis=-1, keepdims=True) + EPSILON)
    normal = center * inv_std
    return (normal, inv_std, round_half(normal * gain_row))


def norm_backward(grad_result, normal, inv_std, gain_row):
    scaled = grad_result * gain_row
    grad_data = inv_std * (
        scaled
        - jnp.mean(scaled, axis=-1, keepdims=True)
        - normal * jnp.mean(scaled * normal, axis=-1, keepdims=True)
    )
    return (grad_data, jnp.sum(grad_result * normal, axis=0))


def gelu_value(pre_act):
    return 0.5 * pre_act * (1.0 + lax.erf(pre_act * ROOT_HALF))


def gelu_slope(pre_act):
    return 0.5 * (1.0 + lax.erf(pre_act * ROOT_HALF)) + pre_act * INV_ROOT_TAU * jnp.exp(
        -0.5 * pre_act * pre_act
    )


def score_table(queries, key_rows):
    return jnp.einsum("bqhd,bkhd->bhqk", queries, key_rows, preferred_element_type=jnp.float32) * (
        1.0 / math.sqrt(HEAD_DIM)
    )


def attention_forward(normed, mats_half, image_count, seq_len):
    head_count = mats_half.shape[2] // HEAD_DIM

    def project(which_mat):
        return round_half(
            jnp.dot(normed, mats_half[which_mat], preferred_element_type=jnp.float32)
        ).reshape(image_count, seq_len, head_count, HEAD_DIM)

    queries = project(0)
    key_rows = project(1)
    value_rows = project(2)
    scores = score_table(queries, key_rows)
    row_peak = jnp.max(scores, axis=-1, keepdims=True)
    log_total = row_peak + jnp.log(jnp.sum(jnp.exp(scores - row_peak), axis=-1, keepdims=True))
    prob_half = round_half(jnp.exp(scores - log_total))
    attn_rows = round_half(
        jnp.einsum("bhqk,bkhd->bqhd", prob_half, value_rows, preferred_element_type=jnp.float32)
    )
    return (
        queries,
        key_rows,
        value_rows,
        log_total,
        attn_rows.reshape(image_count * seq_len, head_count * HEAD_DIM),
    )


def attention_backward(grad_attn_rows, queries, key_rows, value_rows, log_total):
    image_count, seq_len, head_count, head_size = queries.shape
    grad_heads = grad_attn_rows.reshape(image_count, seq_len, head_count, head_size)
    prob_full = jnp.exp(score_table(queries, key_rows) - log_total)
    prob_half = round_half(prob_full)
    grad_prob = jnp.einsum(
        "bqhd,bkhd->bhqk", grad_heads, value_rows, preferred_element_type=jnp.float32
    )
    grad_values = round_half(
        jnp.einsum("bhqk,bqhd->bkhd", prob_half, grad_heads, preferred_element_type=jnp.float32)
    )
    spread = jnp.sum(prob_full * grad_prob, axis=-1, keepdims=True)
    grad_scores = round_half(prob_full * (grad_prob - spread) * (1.0 / math.sqrt(HEAD_DIM)))
    grad_queries = round_half(
        jnp.einsum("bhqk,bkhd->bqhd", grad_scores, key_rows, preferred_element_type=jnp.float32)
    )
    grad_keys = round_half(
        jnp.einsum("bhqk,bqhd->bkhd", grad_scores, queries, preferred_element_type=jnp.float32)
    )
    row_total = image_count * seq_len
    full_width = head_count * head_size
    return (
        grad_queries.reshape(row_total, full_width),
        grad_keys.reshape(row_total, full_width),
        grad_values.reshape(row_total, full_width),
    )


def orthogonalize(matrix):
    current = settle(matrix * lax.rsqrt(jnp.sum(matrix * matrix) + EPSILON))
    for iteration in range(NS_ITERS):
        gram_mat = settle(contract_rows(current, current))
        square = jnp.dot(gram_mat, gram_mat, preferred_element_type=jnp.float32)
        poly_mat = round_half(NEWTON_B * to_single(gram_mat) + NEWTON_C * square)
        current = settle(
            NEWTON_A * to_single(current)
            + jnp.dot(current, poly_mat, preferred_element_type=jnp.float32)
        )
    return current


def orthogonalize_attention(block_mat):
    rows_all, slot_width = block_mat.shape
    sub_blocks = jnp.transpose(block_mat.reshape(rows_all, 2, slot_width // 2), (1, 0, 2))
    solved = jnp.stack([orthogonalize(sub_blocks[which_mat]) for which_mat in range(2)])
    return jnp.transpose(solved, (1, 0, 2)).reshape(rows_all, slot_width)


def empty_block(block_mat):
    return jnp.zeros(block_mat.shape, jnp.bfloat16)


def shards(
    inputs,
    cotangent,
    norm_gains,
    attn_mats,
    router,
    expert_in,
    expert_out,
    moment_gains,
    moment_attn,
    moment_router,
    moment_in,
    moment_out,
    routes,
):
    image_count, seq_len, model_width = inputs.shape
    dp_count = lax.axis_size("dp")
    row_count = image_count * seq_len
    small_plane = jnp.zeros((1, norm_gains.shape[1], attn_mats.shape[2]), jnp.bfloat16)
    small_plane = small_plane.at[0, :, :2].set(round_half(norm_gains).T)
    small_plane = small_plane.at[0, :, 2 : 2 + EF].set(round_half(router))
    packed = lax.all_gather(
        jnp.concatenate([round_half(attn_mats), small_plane], axis=0), "dp", axis=1, tiled=True
    )
    attn_half = packed[:4]
    gains_half = packed[4, :, :2].T
    router_half = packed[4, :, 2 : 2 + EF]
    in_half = lax.all_gather(round_half(expert_in), "dp", axis=1, tiled=True)
    out_half = lax.all_gather(round_half(expert_out), "dp", axis=1, tiled=True)
    gain_one = to_single(gains_half[0])
    gain_two = to_single(gains_half[1])
    row_in = inputs.reshape(row_count, model_width)
    normal_one, inv_one, normed_one = norm_forward(row_in, gain_one)
    queries, key_rows, value_rows, log_total, attn_rows = attention_forward(
        normed_one, attn_half, image_count, seq_len
    )
    attn_part = contract_cols(attn_rows, attn_half[3])
    attn_full = lax.psum(attn_part.astype(jnp.bfloat16), "tensor").astype(jnp.float32)
    middle = row_in + attn_full
    normal_two, inv_two, normed_two = norm_forward(middle, gain_two)
    picked = routes.reshape(row_count, 2)
    one_hot = (picked[:, :, None] == jnp.arange(EF, dtype=jnp.int32)[None, None, :]).astype(
        jnp.float32
    )
    logits = jnp.dot(normed_two, router_half, preferred_element_type=jnp.float32)
    chosen = jnp.sum(logits[:, None, :] * one_hot, axis=2)
    gate_vals = jax.nn.sigmoid(chosen - chosen[:, ::-1])
    gate_table = jnp.sum(gate_vals[:, :, None] * one_hot, axis=1)
    grad_rows = cotangent.reshape(row_count, model_width)
    pre_act = jnp.einsum("td,edf->etf", normed_two, in_half, preferred_element_type=jnp.float32)
    hidden = round_half(gelu_value(pre_act))
    expert_rows = jnp.einsum("etf,edf->etd", hidden, out_half, preferred_element_type=jnp.float32)
    moe_part = jnp.sum(gate_table.T[:, :, None] * expert_rows, axis=0)
    moe_full = lax.psum(moe_part.astype(jnp.bfloat16), "tensor").astype(jnp.float32)
    output_rows = middle + moe_full
    grad_each = jnp.sum(grad_rows[None] * expert_rows, axis=2).T
    grad_choice_part = jnp.sum(grad_each[:, None, :] * one_hot, axis=2)
    grad_expert = round_half(gate_table.T[:, :, None] * grad_rows[None])
    grad_hidden = jnp.einsum(
        "etd,edf->etf", grad_expert, out_half, preferred_element_type=jnp.float32
    )
    grad_pre = round_half(grad_hidden * gelu_slope(pre_act))
    grad_normed_part = jnp.einsum(
        "etf,edf->td", grad_pre, in_half, preferred_element_type=jnp.float32
    )
    grad_in = jnp.einsum("td,etf->edf", normed_two, grad_pre, preferred_element_type=jnp.float32)
    grad_out = jnp.einsum("etd,etf->edf", grad_expert, hidden, preferred_element_type=jnp.float32)
    joined = lax.psum(
        jnp.concatenate([grad_normed_part, grad_choice_part], axis=1).astype(jnp.bfloat16), "tensor"
    ).astype(jnp.float32)
    grad_normed_moe, grad_choice = (joined[:, :model_width], joined[:, model_width:])
    gate_prod = gate_vals[:, 0] * gate_vals[:, 1]
    grad_first = (grad_choice[:, 0] - grad_choice[:, 1]) * gate_prod
    grad_picked = jnp.stack([grad_first, -grad_first], axis=1)
    grad_logits = round_half(jnp.sum(grad_picked[:, :, None] * one_hot, axis=1))
    grad_router = contract_rows(normed_two, grad_logits)
    grad_normed_two = grad_normed_moe + contract_cols(grad_logits, router_half)
    grad_mid_norm, grad_gain_two = norm_backward(grad_normed_two, normal_two, inv_two, gain_two)
    grad_middle = grad_rows + grad_mid_norm
    grad_mid_half = round_half(grad_middle)
    grad_attn_rows = round_half(
        jnp.dot(grad_mid_half, attn_half[3], preferred_element_type=jnp.float32)
    )
    grad_proj_out = contract_rows(grad_mid_half, attn_rows)
    grad_queries, grad_keys, grad_values = attention_backward(
        grad_attn_rows, queries, key_rows, value_rows, log_total
    )
    grad_attn = jnp.stack(
        [
            contract_rows(normed_one, grad_queries),
            contract_rows(normed_one, grad_keys),
            contract_rows(normed_one, grad_values),
            grad_proj_out,
        ]
    )
    grad_normed_one_part = (
        contract_cols(grad_queries, attn_half[0])
        + contract_cols(grad_keys, attn_half[1])
        + contract_cols(grad_values, attn_half[2])
    )
    grad_normed_one = lax.psum(grad_normed_one_part.astype(jnp.bfloat16), "tensor").astype(
        jnp.float32
    )
    grad_in_norm, grad_gain_one = norm_backward(grad_normed_one, normal_one, inv_one, gain_one)
    grad_inputs_rows = grad_middle + grad_in_norm
    gains_cols = jnp.stack([grad_gain_one, grad_gain_two], axis=1)
    small_cols = jnp.concatenate([gains_cols, grad_router], axis=1)
    got_attn, got_in, got_out, got_small = (
        lax.all_to_all(
            grad_attn.astype(jnp.bfloat16), "dp", split_axis=1, concat_axis=0, tiled=True
        ).astype(grad_attn.dtype),
        lax.all_to_all(
            grad_in.astype(jnp.bfloat16), "dp", split_axis=1, concat_axis=0, tiled=True
        ).astype(grad_in.dtype),
        lax.all_to_all(
            grad_out.astype(jnp.bfloat16), "dp", split_axis=1, concat_axis=0, tiled=True
        ).astype(grad_out.dtype),
        lax.all_to_all(
            small_cols[None].astype(jnp.bfloat16), "dp", split_axis=1, concat_axis=0, tiled=True
        ).astype(jnp.float32),
    )
    sum_attn = fold_sources(got_attn, dp_count)
    sum_in = fold_sources(got_in, dp_count)
    sum_out = fold_sources(got_out, dp_count)
    sum_small = fold_sources(got_small, dp_count)[0]
    sum_gains = sum_small[:, :2].T
    sum_router = sum_small[:, 2:]
    small_step = SMALL_RATE / math.sqrt(image_count * dp_count * seq_len)
    moment_gains_new = MOMENTUM * moment_gains + sum_gains
    moment_attn_new = MOMENTUM * moment_attn + sum_attn
    moment_router_new = MOMENTUM * moment_router + sum_router
    moment_in_new = MOMENTUM * moment_in + sum_in
    moment_out_new = MOMENTUM * moment_out + sum_out
    gains_new = norm_gains - small_step * moment_gains_new
    router_new = router - small_step * moment_router_new
    look_attn = sum_attn + MOMENTUM * moment_attn_new
    look_in = sum_in + MOMENTUM * moment_in_new
    look_out = sum_out + MOMENTUM * moment_out_new
    shard_rows = look_in.shape[1]
    slot_width = look_in.shape[2]
    blocks = 2 * EF + 2
    per_owner = -(-blocks // dp_count)
    slot_count = dp_count * per_owner
    slot_list = list(range(blocks))
    block_list = [
        slot_list.index(slot_number) if slot_number in slot_list else blocks
        for slot_number in range(slot_count)
    ]
    slot_of_block = np.array(slot_list)
    block_of_slot = np.array(block_list)
    kind_of_slot = np.where(block_of_slot < 2, 0, np.where(block_of_slot < blocks, 1, 2))
    attn_slots = jnp.transpose(
        jnp.transpose(look_attn, (1, 0, 2)).reshape(shard_rows, 2, slot_width), (1, 0, 2)
    )
    stacked = jnp.concatenate(
        [attn_slots, look_in, look_out, jnp.zeros((1, shard_rows, slot_width), jnp.float32)], axis=0
    )
    outgoing = jnp.take(stacked, jnp.asarray(block_of_slot, dtype=jnp.int32), axis=0)
    arrived = lax.all_to_all(
        for_sending(outgoing), "dp", split_axis=0, concat_axis=1, tiled=True
    ).astype(outgoing.dtype)
    own_index = lax.axis_index("dp")
    kind_table = jnp.asarray(kind_of_slot, dtype=jnp.int32)
    kind_now = kind_table[own_index * per_owner + 0]
    results = [
        lax.switch(kind_now, [orthogonalize_attention, orthogonalize, empty_block], arrived[0])
    ]
    finished = jnp.stack(results)
    returned = lax.all_to_all(
        for_sending(finished), "dp", split_axis=1, concat_axis=0, tiled=True
    ).astype(finished.dtype)
    updates = to_single(jnp.take(returned, jnp.asarray(slot_of_block, dtype=jnp.int32), axis=0))
    update_attn = jnp.transpose(
        jnp.transpose(updates[0:2], (1, 0, 2)).reshape(shard_rows, 4, slot_width // 2), (1, 0, 2)
    )
    attn_new = attn_mats - MUON_RATE * update_attn
    in_new = expert_in - MUON_RATE * updates[2 : EF + 2]
    out_new = expert_out - MUON_RATE * updates[EF + 2 : 2 * EF + 2]
    output = output_rows.reshape(image_count, seq_len, model_width)
    grad_inputs = grad_inputs_rows.reshape(image_count, seq_len, model_width)
    return (
        output,
        grad_inputs,
        sum_gains,
        sum_attn,
        sum_router,
        sum_in,
        sum_out,
        gains_new,
        attn_new,
        router_new,
        in_new,
        out_new,
        moment_gains_new,
        moment_attn_new,
        moment_router_new,
        moment_in_new,
        moment_out_new,
    )


def solution(mesh):
    return jax.shard_map(
        shards,
        mesh=mesh,
        in_specs=(
            P("dp", None, None),
            P("dp", None, None),
            P(None, "dp"),
            P(None, "dp", "tensor"),
            P("dp", None),
            P(None, "dp", "tensor"),
            P(None, "dp", "tensor"),
            P(None, "dp"),
            P(None, "dp", "tensor"),
            P("dp", None),
            P(None, "dp", "tensor"),
            P(None, "dp", "tensor"),
            P("dp", None, None),
        ),
        out_specs=(
            P("dp", None, None),
            P("dp", None, None),
            P(None, "dp"),
            P(None, "dp", "tensor"),
            P("dp", None),
            P(None, "dp", "tensor"),
            P(None, "dp", "tensor"),
            P(None, "dp"),
            P(None, "dp", "tensor"),
            P("dp", None),
            P(None, "dp", "tensor"),
            P(None, "dp", "tensor"),
            P(None, "dp"),
            P(None, "dp", "tensor"),
            P("dp", None),
            P(None, "dp", "tensor"),
            P(None, "dp", "tensor"),
        ),
        check_vma=False,
    )
```

profile of v0, /device:TPU:32, one launch (start us, length us, event | category | flops | bytes accessed | tf_op | source)
XLA Modules:
  0.0 853.9 jit_solution(13263834224516836586)
XLA Ops:
  19.4 121.1 %all-gather.4.cloned.1.call-done = bf16[5,768,192]{2,0,1:T(8,128)(2,1)} async-done(((bf16[5,12,192]{2,0,1:T(8,128)(2,1)}), bf16[5,768,192]{2,0,1:T(8,128)(2,1)}) %all-gather.4.cloned.1.call-update) | async-done | bytes 1474576 | tf_op jit(solution)/shard_map/all_gather | solution.py:191
  142.6 9.2 %fusion.173 = (bf16[1,768,192]{2,0,1:T(2,128)(2,1)}, bf16[1,768,192]{2,0,1:T(2,128)(2,1)}, bf16[1,768,192]{2,0,1:T(2,128)(2,1)S(1)}, bf16[1,768,192]{2,0,1:T(2,128)(2,1)S(1)}) fusion(bf16[5,768,192]{2,0,1:T(8,128)(2,1)} %all-gather.4.cloned.1.call-done), kind=kLoop, calls=%fused_computation.301 | loop fusion | bytes 2359296 | tf_op jit(solution)/shard_map/slice | solution.py:206
  168.9 34.6 %all-reduce.6.cloned.1.call-done = bf16[197,768]{0,1:T(8,128)(2,1)} async-done(((bf16[197,768]{0,1:T(8,128)(2,1)}), bf16[197,768]{0,1:T(8,128)(2,1)}) %all-reduce.6.cloned.1.call-update) | async-done | bytes 302608 | tf_op jit(solution)/shard_map/psum | solution.py:207
  205.4 122.8 %all-gather.6.cloned.1.call-done = bf16[3,768,384]{2,0,1:T(4,128)(2,1)} async-done(((bf16[3,12,384]{2,0,1:T(4,128)(2,1)}), bf16[3,768,384]{2,0,1:T(4,128)(2,1)}) %all-gather.6.cloned.1.call-update) | async-done | bytes 1769488 | tf_op jit(solution)/shard_map/all_gather | solution.py:197
  331.5 117.3 %all-gather.8.cloned.1.call-done = bf16[3,768,384]{2,0,1:T(4,128)(2,1)} async-done(((bf16[3,12,384]{2,0,1:T(4,128)(2,1)}), bf16[3,768,384]{2,0,1:T(4,128)(2,1)}) %all-gather.8.cloned.1.call-update) | async-done | bytes 1769488 | tf_op jit(solution)/shard_map/all_gather | solution.py:198
  448.8 4.0 multiply_reduce_fusion.2
  457.4 38.1 %all-reduce.8.cloned.1.call-done = bf16[197,770]{0,1:T(8,128)(2,1)} async-done(((bf16[197,770]{0,1:T(8,128)(2,1)}), bf16[197,770]{0,1:T(8,128)(2,1)}) %all-reduce.8.cloned.1.call-update) | async-done | bytes 303396 | tf_op jit(solution)/shard_map/psum | solution.py:237
  514.2 12.9 %all-to-all-start.1 = ((bf16[4,768,192]{2,0,1:T(4,128)(2,1)}), bf16[4,768,192]{2,0,1:T(4,128)(2,1)}, u32[]{:S(2)}, u32[]{:S(2)}) async-start(bf16[4,768,192]{2,0,1:T(4,128)(2,1)} %copy.251), calls=%async_computation.1 | async-start | bytes 3145728 | tf_op jit(solution)/shard_map/all_to_all | solution.py:278
  529.1 5.2 copy.253
  534.3 34.5 %all-to-all-done.1 = bf16[4,768,192]{2,0,1:T(4,128)(2,1)} async-done(((bf16[4,768,192]{2,0,1:T(4,128)(2,1)}), bf16[4,768,192]{2,0,1:T(4,128)(2,1)}, u32[]{:S(2)}, u32[]{:S(2)}) %all-to-all-start.1) | async-done | bytes 1179680 | tf_op jit(solution)/shard_map/all_to_all | solution.py:278
  568.8 6.8 all-to-all-start.2
  580.7 51.8 %all-to-all-done.2 = bf16[3,768,384]{2,0,1:T(4,128)(2,1)} async-done(((bf16[3,768,384]{2,0,1:T(4,128)(2,1)}), bf16[3,768,384]{2,0,1:T(4,128)(2,1)}, u32[]{:S(2)}, u32[]{:S(2)}) %all-to-all-start.2) | async-done | bytes 1769504 | tf_op jit(solution)/shard_map/all_to_all | solution.py:281
  632.4 6.5 all-to-all-start.3
  650.3 4.7 reshape.538
  657.6 38.2 %all-to-all-done.3 = bf16[3,768,384]{2,0,1:T(4,128)(2,1)} async-done(((bf16[3,768,384]{2,0,1:T(4,128)(2,1)}), bf16[3,768,384]{2,0,1:T(4,128)(2,1)}, u32[]{:S(2)}, u32[]{:S(2)}) %all-to-all-start.3) | async-done | bytes 1769504 | tf_op jit(solution)/shard_map/all_to_all | solution.py:284
  699.4 4.7 reshape.539
  709.2 6.4 all-to-all-start.4
  723.1 41.8 %all-reduce.10.cloned.1.call-done = (bf16[197,768]{0,1:T(8,128)(2,1)}, bf16[197,768]{0,1:T(8,128)(2,1)}) async-done(((bf16[197,768]{0,1:T(8,128)(2,1)}, bf16[197,768]{0,1:T(8,128)(2,1)}), (bf16[197,768]{0,1:T(8,128)(2,1)}, bf16[197,768]{0,1:T(8,128)(2,1)})) %all-reduce.10.cloned.1.call-update) | async-done | bytes 605200 | tf_op jit(solution)/shard_map/psum | solution.py:223
  768.9 12.8 %all-to-all-start = ((bf16[1,768,5]{2,0,1:T(2,128)(2,1)}), bf16[1,768,5]{2,0,1:T(2,128)(2,1)}, u32[]{:S(2)}, u32[]{:S(2)}) async-start(bf16[1,768,5]{2,0,1:T(2,128)(2,1)} %copy.249), calls=%async_computation | async-start | bytes 786432 | tf_op jit(solution)/shard_map/all_to_all | solution.py:287
  782.6 8.6 %conditional.1 = (bf16[768,384]{0,1:T(8,128)(2,1)S(1)}) conditional(s32[]{:T(128)} %bitcast.63, bf16[64,12,384]{2,1,0:T(8,128)(2,1)S(1)} %all-to-all-done.4, bf16[64,12,384]{2,1,0:T(8,128)(2,1)S(1)} %all-to-all-done.4, () %tuple.25), branch_computations={%region_28.31_spmd, %region_31.0_spmd, %region_33.34_spmd} | conditional | flops 1706655744 | bytes 14450752 | solution.py:335
  796.0 5.1 reduce.33
  803.7 12.9 %all-to-all-start.5 = ((bf16[64,2,2304]{2,1,0:T(2,128)(2,1)}), bf16[64,2,2304]{2,1,0:T(2,128)(2,1)}, u32[]{:S(2)}, u32[]{:S(2)}) async-start(bf16[64,2,2304]{2,1,0:T(2,128)(2,1)} %reshape.565), calls=%async_computation.5 | async-start | bytes 1179648 | tf_op jit(solution)/shard_map/all_to_all | solution.py:338
  822.0 14.9 %all-to-all-done.5 = bf16[64,2,2304]{2,1,0:T(2,128)(2,1)} async-done(((bf16[64,2,2304]{2,1,0:T(2,128)(2,1)}), bf16[64,2,2304]{2,1,0:T(2,128)(2,1)}, u32[]{:S(2)}, u32[]{:S(2)}) %all-to-all-start.5) | async-done | bytes 589856 | tf_op jit(solution)/shard_map/all_to_all | solution.py:338
  836.9 3.8 reshape.566
  (260 shorter events, 118.9 us)
Async XLA Ops:
  7.2 133.3 %all-gather.4.cloned.1.call-start = ((), (), s32[]{:S(2)}) async-start(), calls=%async_computation.6 | async-start | bytes 3194880 | tf_op jit(solution)/shard_map/all_gather | solution.py:191
  15.6 187.9 %all-reduce.6.cloned.1.call-start = ((), (), s32[]{:S(2)}) async-start(), calls=%async_computation.7 | async-start | bytes 786432 | tf_op jit(solution)/shard_map/psum | solution.py:207
  164.2 164.0 %all-gather.6.cloned.1.call-start = ((), (), s32[]{:S(2)}) async-start(), calls=%async_computation.8 | async-start | bytes 2396160 | tf_op jit(solution)/shard_map/all_gather | solution.py:197
  165.0 283.8 %all-gather.8.cloned.1.call-start = ((), (), s32[]{:S(2)}) async-start(), calls=%async_computation.9 | async-start | bytes 2396160 | tf_op jit(solution)/shard_map/all_gather | solution.py:198
  165.7 329.9 %all-reduce.8.cloned.1.call-start = ((), (), s32[]{:S(2)}) async-start(), calls=%async_computation.10 | async-start | bytes 794624 | tf_op jit(solution)/shard_map/psum | solution.py:237
  166.3 286.6 %copy-start.10 = (f32[1,197,768]{2,1,0:T(8,128)}, f32[1,197,768]{2,1,0:T(8,128)S(1)}, u32[]{:S(2)}) copy-start(f32[1,197,768]{2,1,0:T(8,128)S(1)} %copy.306) | copy-start | bytes 1815556
  168.9 36.3 %copy-start.41 = (s32[1,197,2]{1,2,0:T(2,128)S(1)}, s32[1,197,2]{1,2,0:T(2,128)}, u32[]{:S(2)}) copy-start(s32[1,197,2]{1,2,0:T(2,128)} %param.35) | copy-start | bytes 4732
  204.8 291.9 %copy-start.47 = (f32[197]{0:T(256)}, f32[197]{0:T(256)S(1)}, u32[]{:S(2)}) copy-start(f32[197]{0:T(256)S(1)} %add_rsqrt_fusion) | copy-start | bytes 2368
  205.4 247.5 %copy-start.48 = (f32[197,3]{0,1:T(4,128)}, f32[197,3]{0,1:T(4,128)S(1)}, u32[]{:S(2)}) copy-start(f32[197,3]{0,1:T(4,128)S(1)} %select_reduce_fusion.2) | copy-start | bytes 7096
  514.2 54.6 %all-to-all-start.1 = ((bf16[4,768,192]{2,0,1:T(4,128)(2,1)}), bf16[4,768,192]{2,0,1:T(4,128)(2,1)}, u32[]{:S(2)}, u32[]{:S(2)}) async-start(bf16[4,768,192]{2,0,1:T(4,128)(2,1)} %copy.251), calls=%async_computation.1 | async-start | bytes 3145728 | tf_op jit(solution)/shard_map/all_to_all | solution.py:278
  534.3 41.3 %copy-start.11 = (f32[1,197,768]{2,1,0:T(8,128)S(1)}, f32[1,197,768]{2,1,0:T(8,128)}, u32[]{:S(2)}) copy-start(f32[1,197,768]{2,1,0:T(8,128)} %copy-done.10) | copy-start | bytes 1815556
  534.3 41.3 %copy-start.49 = (f32[197,3]{0,1:T(4,128)S(1)}, f32[197,3]{0,1:T(4,128)}, u32[]{:S(2)}) copy-start(f32[197,3]{0,1:T(4,128)} %copy-done.48) | copy-start | bytes 7096
  568.8 63.6 %all-to-all-start.2 = ((bf16[3,768,384]{2,0,1:T(4,128)(2,1)}), bf16[3,768,384]{2,0,1:T(4,128)(2,1)}, u32[]{:S(2)}, u32[]{:S(2)}) async-start(bf16[3,768,384]{2,0,1:T(4,128)(2,1)} %copy.253), calls=%async_computation.2 | async-start | bytes 4718592 | tf_op jit(solution)/shard_map/all_to_all | solution.py:281
  580.7 58.4 %copy-start.57 = (s32[64]{0:T(128)S(1)}, s32[64]{0:T(128)}, u32[]{:S(2)}) copy-start(s32[64]{0:T(128)} %constant.199) | copy-start | bytes 772
  580.7 58.4 %copy-start.27 = (bf16[197,768]{1,0:T(8,128)(2,1)S(1)}, bf16[197,768]{1,0:T(8,128)(2,1)}, u32[]{:S(2)}) copy-start(bf16[197,768]{1,0:T(8,128)(2,1)} %get-tuple-element.173) | copy-start | bytes 907780
  632.4 63.3 %all-to-all-start.3 = ((bf16[3,768,384]{2,0,1:T(4,128)(2,1)}), bf16[3,768,384]{2,0,1:T(4,128)(2,1)}, u32[]{:S(2)}, u32[]{:S(2)}) async-start(bf16[3,768,384]{2,0,1:T(4,128)(2,1)} %copy.255), calls=%async_computation.3 | async-start | bytes 4718592 | tf_op jit(solution)/shard_map/all_to_all | solution.py:284
  657.6 49.2 %copy-start.32 = (f32[3,12,384]{2,1,0:T(8,128)}, f32[3,12,384]{2,1,0:T(8,128)S(1)}, u32[]{:S(2)}) copy-start(f32[3,12,384]{2,1,0:T(8,128)S(1)} %reduce_sum.245) | copy-start | bytes 165892
  709.2 59.7 %all-to-all-start.4 = ((bf16[64,12,384]{2,1,0:T(8,128)(2,1)}), bf16[64,12,384]{2,1,0:T(8,128)(2,1)S(1)}, u32[]{:S(2)}, u32[]{:S(2)}) async-start(bf16[64,12,384]{2,1,0:T(8,128)(2,1)} %gather_fusion), calls=%async_computation.4 | async-start | bytes 1572864 | tf_op jit(solution)/shard_map/all_to_all | solution.py:328
  715.5 49.4 %copy-start.38 = (f32[768]{0:T(1024)S(1)}, f32[768]{0:T(1024)}, u32[]{:S(2)}) copy-start(f32[768]{0:T(1024)} %get-tuple-element.181) | copy-start | bytes 9220
  715.6 49.4 %copy-start.43 = (f32[197]{0:T(256)S(1)}, f32[197]{0:T(256)}, u32[]{:S(2)}) copy-start(f32[197]{0:T(256)} %copy-done.42) | copy-start | bytes 2368
  715.6 49.4 %copy-start.45 = (f32[197]{0:T(256)S(1)}, f32[197]{0:T(256)}, u32[]{:S(2)}) copy-start(f32[197]{0:T(256)} %add_rsqrt_fusion.1) | copy-start | bytes 2368
  715.6 49.4 %all-reduce.10.cloned.1.call-start = ((), (), s32[]{:S(2)}) async-start(), calls=%async_computation.11 | async-start | bytes 1572864 | tf_op jit(solution)/shard_map/psum | solution.py:223
  768.9 34.9 %all-to-all-start = ((bf16[1,768,5]{2,0,1:T(2,128)(2,1)}), bf16[1,768,5]{2,0,1:T(2,128)(2,1)}, u32[]{:S(2)}, u32[]{:S(2)}) async-start(bf16[1,768,5]{2,0,1:T(2,128)(2,1)} %copy.249), calls=%async_computation | async-start | bytes 786432 | tf_op jit(solution)/shard_map/all_to_all | solution.py:287
  803.7 33.1 %all-to-all-start.5 = ((bf16[64,2,2304]{2,1,0:T(2,128)(2,1)}), bf16[64,2,2304]{2,1,0:T(2,128)(2,1)}, u32[]{:S(2)}, u32[]{:S(2)}) async-start(bf16[64,2,2304]{2,1,0:T(2,128)(2,1)} %reshape.565), calls=%async_computation.5 | async-start | bytes 1179648 | tf_op jit(solution)/shard_map/all_to_all | solution.py:338
  (48 other events, 294.1 us)
Sparse Core Ops, SparseCore 0:
  15.7 124.7 all-gather.3
  164.4 39.1 all-reduce.5
  208.4 119.7 all-gather.5
  332.9 115.8 all-gather.7
  456.3 39.2 all-reduce.7
  719.4 45.5 all-reduce.9
where the time goes:
time: 861 us; the launch traced here: 854 us
  waiting for transfers between devices  615 us (71%)
  local copies, waits for them, and re-layouts  75.5 us (9%)
  starting transfers between devices  59 us (7%)
  other arithmetic  45.9 us (5%)
  matrix products  33.5 us (4%)
  between operations  16.3 us (2%)
    all_gather x1, waiting for transfers between devices, shards(): in_half = lax.all_gather(round_half(expert_in), 'dp', axis=1, tiled=True)  123 us
    all_gather x1, waiting for transfers between devices, shards(): lax.all_gather(jnp.concatenate([round_half(attn_mats), small_plane], axis...  121 us
    all_gather x1, waiting for transfers between devices, shards(): out_half = lax.all_gather(round_half(expert_out), 'dp', axis=1, tiled=True)  117 us
    all_to_all x1, waiting for transfers between devices, shards(): lax.all_to_all(grad_in.astype(jnp.bfloat16), 'dp', split_axis=1, concat_a...  51.8 us
    psum x1, waiting for transfers between devices, shards(): lax.psum(moe_part.astype(jnp.bfloat16), 'tensor').astype(jnp.float32)  41.8 us
    all_to_all x1, waiting for transfers between devices, shards(): lax.all_to_all(grad_out.astype(jnp.bfloat16), 'dp', split_axis=1, concat_...  38.2 us
    psum x1, waiting for transfers between devices, shards(): lax.psum(jnp.concatenate([grad_normed_part, grad_choice_part], axis=1).as...  38.1 us
    psum x1, waiting for transfers between devices, shards(): lax.psum(attn_part.astype(jnp.bfloat16), 'tensor').astype(jnp.float32)  34.6 us
  transfers between devices with their start and end apart: 12, of which 10 were waited for; matrix products, arithmetic and copies ran while one was open for 9% of the time, Pallas kernels for 0%

commit v1 on v0

--- a/solution.py
+++ b/solution.py
@@ -18,6 +18,13 @@
 NEWTON_C = 2.0315
 ROOT_HALF = 0.7071067811865476
 INV_ROOT_TAU = 0.3989422804014327
+
+
+def gather_over(array, axis, dim):
+    size = lax.axis_size(axis)
+    pieces = jnp.stack([array for _ in range(size)])
+    pieces = lax.all_to_all(pieces, axis, split_axis=0, concat_axis=0)
+    return jnp.concatenate(pieces, axis=dim)
 
 
 def for_sending(value):
@@ -195,7 +202,7 @@
     gains_half = packed[4, :, :2].T
     router_half = packed[4, :, 2 : 2 + EF]
     in_half = lax.all_gather(round_half(expert_in), "dp", axis=1, tiled=True)
-    out_half = lax.all_gather(round_half(expert_out), "dp", axis=1, tiled=True)
+    out_half = gather_over(round_half(expert_out), "dp", 1)
     gain_one = to_single(gains_half[0])
     gain_two = to_single(gains_half[1])
     row_in = inputs.reshape(row_count, model_width)

time: 861 us -> 749 us (0.87)
  waiting for transfers between devices: 615 us -> 493 us
    all_gather x1 -> x0, waiting for transfers between devices: 117 us -> none  [shards(): out_half = lax.all_gather(round_half(expert_out), 'dp', axis=1, tiled=True)]
    all_gather x1, waiting for transfers between devices: 123 us -> 101 us  [shards(): in_half = lax.all_gather(round_half(expert_in), 'dp', axis=1, tiled=True)]
    all_to_all x0 -> x1, waiting for transfers between devices: none -> 15.9 us  [gather_over(): pieces = lax.all_to_all(pieces, axis, split_axis=0, concat_axis=0)]
    unnamed x134 -> x139, local copies, waits for them, and re-layouts: 23.2 us -> 20.6 us
  transfers between devices with their start and end apart: 12 -> 12, of which waited for: 10 -> 10; matrix products, arithmetic and copies ran while one was open for 9% -> 10% of each run, Pallas kernels for 0% -> 0%
where the time goes in v1:
time: 749 us; the launch traced here: 741 us
  waiting for transfers between devices  493 us (66%)
  local copies, waits for them, and re-layouts  81.6 us (11%)
  starting transfers between devices  67.3 us (9%)
  other arithmetic  44 us (6%)
  matrix products  31.4 us (4%)
  between operations  15.7 us (2%)
  loops' own time  8.62 us (1%)
    all_gather x1, waiting for transfers between devices, shards(): lax.all_gather(jnp.concatenate([round_half(attn_mats), small_plane], axis...  122 us
    all_gather x1, waiting for transfers between devices, shards(): in_half = lax.all_gather(round_half(expert_in), 'dp', axis=1, tiled=True)  101 us
    all_to_all x1, waiting for transfers between devices, shards(): lax.all_to_all(grad_in.astype(jnp.bfloat16), 'dp', split_axis=1, concat_a...  51.9 us
    psum x1, waiting for transfers between devices, shards(): lax.psum(moe_part.astype(jnp.bfloat16), 'tensor').astype(jnp.float32)  41.9 us
    all_to_all x1, waiting for transfers between devices, shards(): lax.all_to_all(grad_out.astype(jnp.bfloat16), 'dp', split_axis=1, concat_...  38.1 us
    psum x1, waiting for transfers between devices, shards(): lax.psum(jnp.concatenate([grad_normed_part, grad_choice_part], axis=1).as...  38.1 us
    all_to_all x1, waiting for transfers between devices, shards(): lax.all_to_all(grad_attn.astype(jnp.bfloat16), 'dp', split_axis=1, concat...  34.5 us
    psum x1, waiting for transfers between devices, shards(): lax.psum(attn_part.astype(jnp.bfloat16), 'tensor').astype(jnp.float32)  33.9 us
  transfers between devices with their start and end apart: 12, of which 10 were waited for; matrix products, arithmetic and copies ran while one was open for 10% of the time, Pallas kernels for 0%

profile of v1, /device:TPU:32, one launch (start us, length us, event | category | flops | bytes accessed | tf_op | source)
XLA Modules:
  0.0 741.4 jit_solution(4374202172980977082)
XLA Ops:
  18.2 122.3 %all-gather.3.cloned.1.call-done = bf16[5,768,192]{2,0,1:T(8,128)(2,1)} async-done(((bf16[5,12,192]{2,0,1:T(8,128)(2,1)}), bf16[5,768,192]{2,0,1:T(8,128)(2,1)}) %all-gather.3.cloned.1.call-update) | async-done | bytes 1474576 | tf_op jit(solution)/shard_map/all_gather | solution.py:198
  143.7 9.1 %fusion.170 = (bf16[1,768,192]{2,0,1:T(2,128)(2,1)S(1)}, bf16[1,768,192]{2,0,1:T(2,128)(2,1)S(1)}, bf16[1,768,192]{2,0,1:T(2,128)(2,1)S(1)}, bf16[1,768,192]{2,0,1:T(2,128)(2,1)}) fusion(bf16[5,768,192]{2,0,1:T(8,128)(2,1)} %all-gather.3.cloned.1.call-done), kind=kLoop, calls=%fused_computation.297 | loop fusion | bytes 2359296 | tf_op jit(solution)/shard_map/slice | solution.py:213
  164.6 8.5 %all-to-all-start = ((bf16[64,3,12,384]{3,2,1,0:T(8,128)(2,1)}), bf16[64,3,12,384]{3,2,1,0:T(8,128)(2,1)}, u32[]{:S(2)}, u32[]{:S(2)}) async-start(bf16[64,3,12,384]{3,2,1,0:T(8,128)(2,1)} %stack.27), calls=%async_computation | async-start | bytes 4718592 | tf_op jit(solution)/shard_map/all_to_all | solution.py:26
  176.7 33.9 %all-reduce.6.cloned.1.call-done = bf16[197,768]{0,1:T(8,128)(2,1)} async-done(((bf16[197,768]{0,1:T(8,128)(2,1)}), bf16[197,768]{0,1:T(8,128)(2,1)}) %all-reduce.6.cloned.1.call-update) | async-done | bytes 302608 | tf_op jit(solution)/shard_map/psum | solution.py:214
  212.4 15.9 %all-to-all-done = bf16[64,3,12,384]{3,2,1,0:T(8,128)(2,1)} async-done(((bf16[64,3,12,384]{3,2,1,0:T(8,128)(2,1)}), bf16[64,3,12,384]{3,2,1,0:T(8,128)(2,1)}, u32[]{:S(2)}, u32[]{:S(2)}) %all-to-all-start) | async-done | bytes 1769504 | tf_op jit(solution)/shard_map/all_to_all | solution.py:26
  231.6 3.9 reshape.535
  235.5 101.3 %all-gather.5.cloned.1.call-done = bf16[3,768,384]{2,0,1:T(4,128)(2,1)} async-done(((bf16[3,12,384]{2,0,1:T(4,128)(2,1)}), bf16[3,768,384]{2,0,1:T(4,128)(2,1)}) %all-gather.5.cloned.1.call-update) | async-done | bytes 1769488 | tf_op jit(solution)/shard_map/all_gather | solution.py:204
  345.7 38.1 %all-reduce.8.cloned.1.call-done = bf16[197,770]{0,1:T(8,128)(2,1)} async-done(((bf16[197,770]{0,1:T(8,128)(2,1)}), bf16[197,770]{0,1:T(8,128)(2,1)}) %all-reduce.8.cloned.1.call-update) | async-done | bytes 303396 | tf_op jit(solution)/shard_map/psum | solution.py:244
  402.0 12.9 %all-to-all-start.2 = ((bf16[4,768,192]{2,0,1:T(4,128)(2,1)}), bf16[4,768,192]{2,0,1:T(4,128)(2,1)}, u32[]{:S(2)}, u32[]{:S(2)}) async-start(bf16[4,768,192]{2,0,1:T(4,128)(2,1)} %copy.241), calls=%async_computation.2 | async-start | bytes 3145728 | tf_op jit(solution)/shard_map/all_to_all | solution.py:285
  416.9 5.2 copy.243
  422.1 34.5 %all-to-all-done.2 = bf16[4,768,192]{2,0,1:T(4,128)(2,1)} async-done(((bf16[4,768,192]{2,0,1:T(4,128)(2,1)}), bf16[4,768,192]{2,0,1:T(4,128)(2,1)}, u32[]{:S(2)}, u32[]{:S(2)}) %all-to-all-start.2) | async-done | bytes 1179680 | tf_op jit(solution)/shard_map/all_to_all | solution.py:285
  456.6 6.8 all-to-all-start.3
  468.3 51.9 %all-to-all-done.3 = bf16[3,768,384]{2,0,1:T(4,128)(2,1)} async-done(((bf16[3,768,384]{2,0,1:T(4,128)(2,1)}), bf16[3,768,384]{2,0,1:T(4,128)(2,1)}, u32[]{:S(2)}, u32[]{:S(2)}) %all-to-all-start.3) | async-done | bytes 1769504 | tf_op jit(solution)/shard_map/all_to_all | solution.py:288
  520.2 6.5 all-to-all-start.4
  538.1 4.7 reshape.548
  545.4 38.1 %all-to-all-done.4 = bf16[3,768,384]{2,0,1:T(4,128)(2,1)} async-done(((bf16[3,768,384]{2,0,1:T(4,128)(2,1)}), bf16[3,768,384]{2,0,1:T(4,128)(2,1)}, u32[]{:S(2)}, u32[]{:S(2)}) %all-to-all-start.4) | async-done | bytes 1769504 | tf_op jit(solution)/shard_map/all_to_all | solution.py:291
  587.2 4.7 reshape.549
  597.0 6.5 all-to-all-start.5
  611.1 41.9 %all-reduce.10.cloned.1.call-done = (bf16[197,768]{0,1:T(8,128)(2,1)}, bf16[197,768]{0,1:T(8,128)(2,1)}) async-done(((bf16[197,768]{0,1:T(8,128)(2,1)}, bf16[197,768]{0,1:T(8,128)(2,1)}), (bf16[197,768]{0,1:T(8,128)(2,1)}, bf16[197,768]{0,1:T(8,128)(2,1)})) %all-reduce.10.cloned.1.call-update) | async-done | bytes 605200 | tf_op jit(solution)/shard_map/psum | solution.py:230
  656.8 12.8 %all-to-all-start.1 = ((bf16[1,768,5]{2,0,1:T(2,128)(2,1)}), bf16[1,768,5]{2,0,1:T(2,128)(2,1)}, u32[]{:S(2)}, u32[]{:S(2)}) async-start(bf16[1,768,5]{2,0,1:T(2,128)(2,1)} %copy.239), calls=%async_computation.1 | async-start | bytes 786432 | tf_op jit(solution)/shard_map/all_to_all | solution.py:294
  670.6 8.7 %conditional.1 = (bf16[768,384]{0,1:T(8,128)(2,1)S(1)}) conditional(s32[]{:T(128)} %bitcast.64, bf16[64,12,384]{2,1,0:T(8,128)(2,1)S(1)} %all-to-all-done.5, bf16[64,12,384]{2,1,0:T(8,128)(2,1)S(1)} %all-to-all-done.5, () %tuple.25), branch_computations={%region_28.31_spmd, %region_31.0_spmd, %region_33.34_spmd} | conditional | flops 1706655744 | bytes 14450752 | solution.py:342
  684.1 5.1 reduce.33
  691.8 12.9 %all-to-all-start.6 = ((bf16[64,2,2304]{2,1,0:T(2,128)(2,1)}), bf16[64,2,2304]{2,1,0:T(2,128)(2,1)}, u32[]{:S(2)}, u32[]{:S(2)}) async-start(bf16[64,2,2304]{2,1,0:T(2,128)(2,1)} %reshape.575), calls=%async_computation.6 | async-start | bytes 1179648 | tf_op jit(solution)/shard_map/all_to_all | solution.py:345
  710.1 14.9 %all-to-all-done.6 = bf16[64,2,2304]{2,1,0:T(2,128)(2,1)} async-done(((bf16[64,2,2304]{2,1,0:T(2,128)(2,1)}), bf16[64,2,2304]{2,1,0:T(2,128)(2,1)}, u32[]{:S(2)}, u32[]{:S(2)}) %all-to-all-start.6) | async-done | bytes 589856 | tf_op jit(solution)/shard_map/all_to_all | solution.py:345
  (268 shorter events, 124.7 us)
Async XLA Ops:
  7.2 133.3 %all-gather.3.cloned.1.call-start = ((), (), s32[]{:S(2)}) async-start(), calls=%async_computation.7 | async-start | bytes 3194880 | tf_op jit(solution)/shard_map/all_gather | solution.py:198
  15.6 194.9 %all-reduce.6.cloned.1.call-start = ((), (), s32[]{:S(2)}) async-start(), calls=%async_computation.8 | async-start | bytes 786432 | tf_op jit(solution)/shard_map/psum | solution.py:214
  18.1 634.9 %copy-start.43 = (f32[197]{0:T(256)}, f32[197]{0:T(256)S(1)}, u32[]{:S(2)}) copy-start(f32[197]{0:T(256)S(1)} %broadcast_multiply_fusion.5) | copy-start | bytes 2368
  18.2 134.6 %copy-start.48 = (f32[197]{0:T(256)}, f32[197]{0:T(256)S(1)}, u32[]{:S(2)}) copy-start(f32[197]{0:T(256)S(1)} %add_rsqrt_fusion.1) | copy-start | bytes 2368
  164.6 63.7 %all-to-all-start = ((bf16[64,3,12,384]{3,2,1,0:T(8,128)(2,1)}), bf16[64,3,12,384]{3,2,1,0:T(8,128)(2,1)}, u32[]{:S(2)}, u32[]{:S(2)}) async-start(bf16[64,3,12,384]{3,2,1,0:T(8,128)(2,1)} %stack.27), calls=%async_computation | async-start | bytes 4718592 | tf_op jit(solution)/shard_map/all_to_all | solution.py:26
  173.1 163.7 %all-gather.5.cloned.1.call-start = ((), (), s32[]{:S(2)}) async-start(), calls=%async_computation.9 | async-start | bytes 2396160 | tf_op jit(solution)/shard_map/all_gather | solution.py:204
  173.8 210.0 %all-reduce.8.cloned.1.call-start = ((), (), s32[]{:S(2)}) async-start(), calls=%async_computation.10 | async-start | bytes 794624 | tf_op jit(solution)/shard_map/psum | solution.py:244
  174.1 167.0 %copy-start.7 = (f32[1,197,768]{2,1,0:T(8,128)}, f32[1,197,768]{2,1,0:T(8,128)S(1)}, u32[]{:S(2)}) copy-start(f32[1,197,768]{2,1,0:T(8,128)S(1)} %copy.290) | copy-start | bytes 1815556
  211.7 173.3 %copy-start.45 = (f32[197]{0:T(256)}, f32[197]{0:T(256)S(1)}, u32[]{:S(2)}) copy-start(f32[197]{0:T(256)S(1)} %broadcast_multiply_fusion.4) | copy-start | bytes 2368
  211.9 173.1 %copy-start.51 = (f32[197]{0:T(256)}, f32[197]{0:T(256)S(1)}, u32[]{:S(2)}) copy-start(f32[197]{0:T(256)S(1)} %add_rsqrt_fusion) | copy-start | bytes 2368
  212.4 128.7 %copy-start.52 = (f32[197,3]{0,1:T(4,128)}, f32[197,3]{0,1:T(4,128)S(1)}, u32[]{:S(2)}) copy-start(f32[197,3]{0,1:T(4,128)S(1)} %select_reduce_fusion.2) | copy-start | bytes 7096
  402.0 54.6 %all-to-all-start.2 = ((bf16[4,768,192]{2,0,1:T(4,128)(2,1)}), bf16[4,768,192]{2,0,1:T(4,128)(2,1)}, u32[]{:S(2)}, u32[]{:S(2)}) async-start(bf16[4,768,192]{2,0,1:T(4,128)(2,1)} %copy.241), calls=%async_computation.2 | async-start | bytes 3145728 | tf_op jit(solution)/shard_map/all_to_all | solution.py:285
  422.1 41.3 %copy-start.8 = (f32[1,197,768]{2,1,0:T(8,128)S(1)}, f32[1,197,768]{2,1,0:T(8,128)}, u32[]{:S(2)}) copy-start(f32[1,197,768]{2,1,0:T(8,128)} %copy-done.7) | copy-start | bytes 1815556
  422.1 41.3 %copy-start.53 = (f32[197,3]{0,1:T(4,128)S(1)}, f32[197,3]{0,1:T(4,128)}, u32[]{:S(2)}) copy-start(f32[197,3]{0,1:T(4,128)} %copy-done.52) | copy-start | bytes 7096
  456.6 63.7 %all-to-all-start.3 = ((bf16[3,768,384]{2,0,1:T(4,128)(2,1)}), bf16[3,768,384]{2,0,1:T(4,128)(2,1)}, u32[]{:S(2)}, u32[]{:S(2)}) async-start(bf16[3,768,384]{2,0,1:T(4,128)(2,1)} %copy.243), calls=%async_computation.3 | async-start | bytes 4718592 | tf_op jit(solution)/shard_map/all_to_all | solution.py:288
  468.3 58.5 %copy-start.61 = (s32[64]{0:T(128)S(1)}, s32[64]{0:T(128)}, u32[]{:S(2)}) copy-start(s32[64]{0:T(128)} %constant.199) | copy-start | bytes 772
  468.3 58.5 %copy-start.30 = (bf16[197,768]{1,0:T(8,128)(2,1)S(1)}, bf16[197,768]{1,0:T(8,128)(2,1)}, u32[]{:S(2)}) copy-start(bf16[197,768]{1,0:T(8,128)(2,1)} %get-tuple-element.173) | copy-start | bytes 907780
  520.2 63.3 %all-to-all-start.4 = ((bf16[3,768,384]{2,0,1:T(4,128)(2,1)}), bf16[3,768,384]{2,0,1:T(4,128)(2,1)}, u32[]{:S(2)}, u32[]{:S(2)}) async-start(bf16[3,768,384]{2,0,1:T(4,128)(2,1)} %copy.245), calls=%async_computation.4 | async-start | bytes 4718592 | tf_op jit(solution)/shard_map/all_to_all | solution.py:291
  545.4 49.2 %copy-start.35 = (f32[3,12,384]{2,1,0:T(8,128)}, f32[3,12,384]{2,1,0:T(8,128)S(1)}, u32[]{:S(2)}) copy-start(f32[3,12,384]{2,1,0:T(8,128)S(1)} %reduce_sum.245) | copy-start | bytes 165892
  597.0 59.8 %all-to-all-start.5 = ((bf16[64,12,384]{2,1,0:T(8,128)(2,1)}), bf16[64,12,384]{2,1,0:T(8,128)(2,1)S(1)}, u32[]{:S(2)}, u32[]{:S(2)}) async-start(bf16[64,12,384]{2,1,0:T(8,128)(2,1)} %gather_fusion), calls=%async_computation.5 | async-start | bytes 1572864 | tf_op jit(solution)/shard_map/all_to_all | solution.py:335
  603.5 49.4 %copy-start.49 = (f32[197]{0:T(256)S(1)}, f32[197]{0:T(256)}, u32[]{:S(2)}) copy-start(f32[197]{0:T(256)} %copy-done.48) | copy-start | bytes 2368
  603.5 49.4 %all-reduce.10.cloned.1.call-start = ((), (), s32[]{:S(2)}) async-start(), calls=%async_computation.11 | async-start | bytes 1572864 | tf_op jit(solution)/shard_map/psum | solution.py:230
  656.8 35.0 %all-to-all-start.1 = ((bf16[1,768,5]{2,0,1:T(2,128)(2,1)}), bf16[1,768,5]{2,0,1:T(2,128)(2,1)}, u32[]{:S(2)}, u32[]{:S(2)}) async-start(bf16[1,768,5]{2,0,1:T(2,128)(2,1)} %copy.239), calls=%async_computation.1 | async-start | bytes 786432 | tf_op jit(solution)/shard_map/all_to_all | solution.py:294
  691.8 33.1 %all-to-all-start.6 = ((bf16[64,2,2304]{2,1,0:T(2,128)(2,1)}), bf16[64,2,2304]{2,1,0:T(2,128)(2,1)}, u32[]{:S(2)}, u32[]{:S(2)}) async-start(bf16[64,2,2304]{2,1,0:T(2,128)(2,1)} %reshape.575), calls=%async_computation.6 | async-start | bytes 1179648 | tf_op jit(solution)/shard_map/all_to_all | solution.py:345
  (51 other events, 310.6 us)
Sparse Core Ops, SparseCore 0:
  15.7 124.7 all-gather.2
  163.0 47.4 all-reduce.5
  215.4 121.3 all-gather.4
  344.5 39.2 all-reduce.7
  607.3 45.5 all-reduce.9
